TPU v7x, 512 devices: a whole 4x4x16 slice. The times are simulated.
512 devices in a mesh: gx: 32 (over z, core), vert: 16 (over y, x).
Axes of the slice: x: 4, y: 4, z: 16, core: 2. Of those that a mesh axis runs over, the one named last changes fastest.
Arguments:
- distribution: float32 [4096, 32, 256], P('vert', 'gx'), may hold values from -6 to 6
- relax_rate: float32 [32, 256], P('gx'), may hold values from 0.3 to 3
- node_weight: float32 [4096], P('vert'), may hold values from 0.05 to 1
- kernel_tiles: bfloat16 [32, 128, 1536], P('vert'), may hold values from -0.15625 to 0.15625
- tile_cols: int32 [32, 12], P('vert'), may hold values from 0 to 31, as said below
Outputs:
- new_distribution: float32 [4096, 32, 256], P('vert', 'gx')
Inputs may be any that keep to these rules, and one draw needn't show every extreme that they name: `tile_cols`: row block r lists its own block r first; the 12 column blocks listed for one row block are distinct.
All inputs are finite; a program needn't handle non-finite values.
Results may differ from a plain program's by a relative error of at most 0.0021.
Values may be sent and summed in bfloat16 or wider, within the bound.
No kernel may reach another device: no remote copies, remote signals or barrier semaphores. Data moves between devices by JAX's collectives and lax.ppermute only.
A program may use at most 64 MiB of HBM per device.

v0:
```python
import jax
import jax.numpy as jnp
from jax import lax
from jax.sharding import PartitionSpec as P

Q = 16
TILE = 128
NZ = 4
STEPS = 2
V = 4096
RBLK = 32
COURANT_SCALE = 0.3
KERNEL_STEP = 0.5
PRECISE = lax.Precision.HIGHEST


def extended(block, sides, width):
    for axis, dim in sides:
        count = lax.axis_size(axis)
        forward = [(i, i + 1) for i in range(count - 1)]
        forward.append((count - 1, 0))
        backward = [(target, source) for source, target in forward]
        low = lax.ppermute(
            lax.slice_in_dim(block, block.shape[dim] - width, None, axis=dim), axis, forward
        )
        high = lax.ppermute(lax.slice_in_dim(block, 0, width, axis=dim), axis, backward)
        block = jnp.concatenate([low, block, high], axis=dim)
    return block


def node_components(first_node, node_count):
    node_index = first_node + jnp.arange(node_count, dtype=jnp.int32)
    middle = (Q - 1) / 2.0
    speed_x = ((node_index % Q).astype(jnp.float32) - middle) / middle
    speed_y = ((node_index // Q % Q).astype(jnp.float32) - middle) / middle
    speed_z = ((node_index // (Q * Q)).astype(jnp.float32) - middle) / middle
    courant = COURANT_SCALE * jnp.stack([speed_x, speed_y, speed_z])
    squares = speed_x * speed_x + speed_y * speed_y + speed_z * speed_z
    invariants = jnp.stack([jnp.ones_like(speed_x), speed_x, speed_y, speed_z, squares])
    return (courant, invariants)


def gram_inverse(weighted, invariants):
    gram_matrix = jnp.dot(weighted, invariants.T, precision=PRECISE)
    factor = jnp.linalg.cholesky(gram_matrix)
    return jax.scipy.linalg.cho_solve((factor, True), jnp.eye(5, dtype=gram_matrix.dtype))


def advect(source, lower_x, upper_x, courant):
    plane_size = source.shape[-1]
    z_index = jnp.arange(plane_size, dtype=jnp.int32) % NZ
    lower_y = jnp.roll(source, NZ, axis=-1)
    upper_y = jnp.roll(source, -NZ, axis=-1)
    lower_z = jnp.where(
        z_index == 0, jnp.roll(source, 1 - NZ, axis=-1), jnp.roll(source, 1, axis=-1)
    )
    upper_z = jnp.where(
        z_index == NZ - 1, jnp.roll(source, NZ - 1, axis=-1), jnp.roll(source, -1, axis=-1)
    )
    total_flux = jnp.zeros_like(source)
    for component, below, above in (
        (0, lower_x, upper_x),
        (1, lower_y, upper_y),
        (2, lower_z, upper_z),
    ):
        node_speed = courant[component][:, None, None]
        total_flux = (
            total_flux
            + jnp.maximum(node_speed, 0.0) * (source - below)
            + jnp.minimum(node_speed, 0.0) * (above - source)
        )
    return source - total_flux


def apply_kernel(blocks, tile_rows, column_lists):
    cell_count = blocks.shape[-1]

    def one_block(tile_pair):
        tile_row, column_list = tile_pair
        picked = jnp.take(blocks, column_list, axis=0).reshape(-1, cell_count)
        return jnp.dot(tile_row, picked, preferred_element_type=jnp.float32)

    return lax.map(one_block, (tile_rows, column_lists))


def per_device(distribution, relax_rate, node_weight, kernel_tiles, tile_cols):
    node_local, slab_depth, plane_cells = distribution.shape
    cell_count = slab_depth * plane_cells
    first_node = lax.axis_index("vert") * node_local
    courant, invariants = node_components(first_node, node_local)
    all_weights = lax.all_gather(node_weight, "vert", axis=0, tiled=True)
    all_speeds, all_invariants = node_components(0, V)
    all_weighted = all_invariants * all_weights[None, :]
    inverse = gram_inverse(all_weighted, all_invariants)
    relax_share = relax_rate / (1.0 + relax_rate)
    current = distribution
    for step_index in range(STEPS):
        rounded = current.astype(jnp.bfloat16)
        padded = extended(current, (("gx", 1),), 1)
        lower_x = padded[:, :-2]
        upper_x = padded[:, 2:]
        advected = advect(current, lower_x, upper_x, courant)
        gathered = lax.all_gather(
            rounded.reshape(node_local, cell_count), "vert", axis=0, tiled=True
        )
        kernel_term = apply_kernel(
            gathered.reshape(RBLK, TILE, cell_count), kernel_tiles, tile_cols
        )
        explicit = advected + KERNEL_STEP * kernel_term.reshape(current.shape)
        local_weighted = invariants * node_weight[None, :]
        partial_moments = jnp.dot(
            local_weighted, explicit.reshape(node_local, cell_count), precision=PRECISE
        )
        moments = lax.psum(partial_moments, "vert")
        coeffs = jnp.dot(inverse, moments, precision=PRECISE)
        equilibrium = jnp.dot(invariants.T, coeffs, precision=PRECISE).reshape(current.shape)
        current = explicit - relax_share[None] * (explicit - equilibrium)
    return current


def solution(mesh):
    placed = (
        P("vert", "gx", None),
        P("gx", None),
        P("vert"),
        P("vert", None, None),
        P("vert", None),
    )
    return jax.shard_map(
        per_device, mesh=mesh, in_specs=placed, out_specs=P("vert", "gx", None), check_vma=False
    )
```

profile of v0, /device:TPU:32, one launch (start us, length us, event | category | flops | bytes accessed | tf_op | source)
XLA Modules:
  0.0 240.1 jit_solution(10722678696788781217)
XLA Ops:
  6.5 1.1 copy.54
  7.6 0.5 collective-permute-start
  8.1 1.6 copy.68
  10.2 23.6 %all-gather.2 = f32[16,1,256]{2,1,0:T(1,128)S(1)} all-gather(f32[1,1,256]{2,1,0:T(1,128)} %bitcast.109), channel_id=1, replica_groups=mesh['gx'=32,'vert'=16] {'vert'}, dimensions={0}, use_global_device_ids=true | all-gather | bytes 17408 | tf_op jit(solution)/shard_map/all_gather | solution.py:91
  33.8 0.4 fusion.44
  34.2 0.5 cholesky.17
  34.8 0.6 compare_reduce_fusion
  35.4 0.6 fusion.59
  36.1 0.4 custom-call.10
  36.6 0.7 add_divide_fusion
  37.7 0.7 fusion.82
  38.5 36.6 %all-gather.6.cloned.1.call-done = bf16[4096,1,256]{2,0,1:T(8,128)(2,1)} async-done(((bf16[256,1,256]{2,0,1:T(8,128)(2,1)}), bf16[4096,1,256]{2,0,1:T(8,128)(2,1)}) %all-gather.6.cloned.1.call-update) | async-done | bytes 2097168 | tf_op jit(solution)/shard_map/all_gather | solution.py:103
  75.1 5.3 %while.20 = (s32[]{:T(128)}, f32[2,128,256]{2,1,0:T(8,128)S(1)}, bf16[2,128,1536]{2,1,0:T(8,128)(2,1)S(1)}, s32[2,12]{1,0:T(2,128)S(1)}, bf16[32,128,256]{2,1,0:T(8,128)(2,1)}, /*index=5*/s32[]{:T(128)}) while((s32[]{:T(128)}, f32[2,128,256]{2,1,0:T(8,128)S(1)}, bf16[2,128,1536]{2,1,0:T(8,128)(2,1)S(1)}, s32[2,12]{1,0:T(2,128)S(1)}, ...), condition=%wide.region_1.3_spmd, body=%wide.region_0.2_spmd.sunk | while | flops 101057608 | bytes 4461865 | solution.py:83
  75.1 2.2 gather_fusion
  77.5 0.3 fusion.111
  77.8 2.2 gather_fusion
  80.6 1.4 fusion.22
  82.3 38.7 %psum.14 = f32[5,256]{1,0:T(8,128)S(1)} all-reduce(f32[5,256]{1,0:T(8,128)S(1)} %fusion.42), channel_id=1, replica_groups=mesh['gx'=32,'vert'=16] {'vert'}, use_global_device_ids=true, to_apply=%region_4.6 | all-reduce | flops 1280 | bytes 10240 | tf_op jit(solution)/shard_map/psum | solution.py:114
  121.1 1.1 fusion.88
  122.3 0.5 collective-permute-start.2
  122.9 0.7 fusion.79
  123.6 58.2 %all-gather.8.cloned.1.call-done = bf16[4096,1,256]{0,2,1:T(8,128)(2,1)} async-done(((bf16[256,1,256]{0,2,1:T(8,128)(2,1)}), bf16[4096,1,256]{0,2,1:T(8,128)(2,1)}) %all-gather.8.cloned.1.call-update) | async-done | bytes 2097168 | tf_op jit(solution)/shard_map/all_gather | solution.py:103
  181.8 4.1 %copy.65 = bf16[4096,1,256]{2,0,1:T(8,128)(2,1)} copy(bf16[4096,1,256]{0,2,1:T(8,128)(2,1)} %all-gather.8.cloned.1.call-done) | data formatting | bytes 4194304 | tf_op jit(solution)/shard_map/while | solution.py:83
  185.9 5.3 %while.21 = (s32[]{:T(128)}, f32[2,128,256]{2,1,0:T(8,128)S(1)}, bf16[2,128,1536]{2,1,0:T(8,128)(2,1)S(1)}, s32[2,12]{1,0:T(2,128)S(1)}, bf16[32,128,256]{2,1,0:T(8,128)(2,1)}, /*index=5*/s32[]{:T(128)}) while((s32[]{:T(128)}, f32[2,128,256]{2,1,0:T(8,128)S(1)}, bf16[2,128,1536]{2,1,0:T(8,128)(2,1)S(1)}, s32[2,12]{1,0:T(2,128)S(1)}, ...), condition=%wide.region_6.8_spmd, body=%wide.region_5.7_spmd.sunk | while | flops 101057608 | bytes 4461865 | solution.py:83
  186.0 2.2 gather_fusion.1
  188.3 0.3 fusion.114
  188.6 2.2 gather_fusion.1
  191.0 0.3 fusion.114
  191.4 1.4 fusion.34
  193.1 38.7 %psum.15 = f32[5,256]{1,0:T(8,128)S(1)} all-reduce(f32[5,256]{1,0:T(8,128)S(1)} %fusion.40), channel_id=1, replica_groups=mesh['gx'=32,'vert'=16] {'vert'}, use_global_device_ids=true, to_apply=%region_7.9 | all-reduce | flops 1280 | bytes 10240 | tf_op jit(solution)/shard_map/psum | solution.py:114
  231.9 0.4 fusion.15
  232.4 0.8 copy.62
  (65 shorter events, 3.2 us)
Async XLA Ops:
  6.5 68.5 %all-gather.6.cloned.1.call-start = ((), (), s32[]{:S(2)}) async-start(), calls=%async_computation | async-start | bytes 2228224 | tf_op jit(solution)/shard_map/all_gather | solution.py:103
  7.6 73.0 %collective-permute-start.1 = (f32[256,1,256]{0,2,1:T(8,128)S(1)}, f32[256,1,256]{0,2,1:T(8,128)}, u32[]{:S(2)}, u32[]{:S(2)}) collective-permute-start(f32[256,1,256]{0,2,1:T(8,128)S(1)} %copy.54), channel_id=1, source_target_pairs={{16,0},{32,16},{48,32},{64,48},{80,64},{96,80},{112,96},{128,112},... | collective-permute-start | bytes 786440 | tf_op jit(solution)/shard_map/ppermute | solution.py:26
  7.6 73.0 %collective-permute-start = (f32[256,1,256]{0,2,1:T(8,128)S(1)}, f32[256,1,256]{0,2,1:T(8,128)}, u32[]{:S(2)}, u32[]{:S(2)}) collective-permute-start(f32[256,1,256]{0,2,1:T(8,128)S(1)} %copy.54), channel_id=1, source_target_pairs={{0,16},{16,32},{32,48},{48,64},{64,80},{80,96},{96,112},{112,128},... | collective-permute-start | bytes 786440 | tf_op jit(solution)/shard_map/ppermute | solution.py:23
  9.8 65.3 %copy-start = (bf16[2,128,1536]{2,1,0:T(8,128)(2,1)S(1)}, bf16[2,128,1536]{2,1,0:T(8,128)(2,1)}, u32[]{:S(2)}) copy-start(bf16[2,128,1536]{2,1,0:T(8,128)(2,1)} %param.14) | copy-start | bytes 2359300
  9.8 65.3 %copy-start.1 = (s32[2,12]{1,0:T(2,128)S(1)}, s32[2,12]{1,0:T(2,128)}, u32[]{:S(2)}) copy-start(s32[2,12]{1,0:T(2,128)} %param.15) | copy-start | bytes 292
  9.8 172.0 %all-gather.8.cloned.1.call-start = ((), (), s32[]{:S(2)}) async-start(), calls=%async_computation.1 | async-start | bytes 2228224 | tf_op jit(solution)/shard_map/all_gather | solution.py:103
  80.4 1.6 copy-start.2
  122.2 69.2 %collective-permute-start.3 = (f32[256,1,256]{0,2,1:T(8,128)S(1)}, f32[256,1,256]{0,2,1:T(8,128)}, u32[]{:S(2)}, u32[]{:S(2)}) collective-permute-start(f32[256,1,256]{0,2,1:T(8,128)S(1)} %get-tuple-element.127), channel_id=1, source_target_pairs={{16,0},{32,16},{48,32},{64,48},{80,64},{96,80},{112,96},{128,112},... | collective-permute-start | bytes 786440 | tf_op jit(solution)/shard_map/ppermute | solution.py:26
  122.3 69.2 %collective-permute-start.2 = (f32[256,1,256]{0,2,1:T(8,128)S(1)}, f32[256,1,256]{0,2,1:T(8,128)}, u32[]{:S(2)}, u32[]{:S(2)}) collective-permute-start(f32[256,1,256]{0,2,1:T(8,128)S(1)} %get-tuple-element.127), channel_id=1, source_target_pairs={{0,16},{16,32},{32,48},{48,64},{64,80},{80,96},{96,112},{112,128},... | collective-permute-start | bytes 786440 | tf_op jit(solution)/shard_map/ppermute | solution.py:23
Sparse Core Ops, SparseCore 0:
  10.4 64.6 all-gather.5
  122.3 59.4 all-gather.7
where the time goes:
time: 241 us; the launch traced here: 240 us
  blocking collectives  101 us (42%)
  waiting for transfers between devices  94.9 us (39%)
  local copies, waits for them, and re-layouts  18.6 us (8%)
  between operations  13.7 us (6%)
  other arithmetic  6.55 us (3%)
  matrix products  4.07 us (2%)
    all_gather x2, waiting for transfers between devices, per_device(): lax.all_gather(rounded.reshape(node_local, cell_count), 'vert', axis=0, t...  94.8 us
    psum x2, blocking collectives, per_device(): moments = lax.psum(partial_moments, 'vert')  77.4 us
    all_gather x1, blocking collectives, per_device(): all_weights = lax.all_gather(node_weight, 'vert', axis=0, tiled=True)  23.6 us
    gather x4, local copies, waits for them, and re-layouts, one_block(): picked = jnp.take(blocks, column_list, axis=0).reshape(-1, cell_count)  8.75 us
  transfers between devices with their start and end apart: 6, of which 2 were waited for; matrix products, arithmetic and copies ran while one was open for 9% of the time, Pallas kernels for 0%

commit v1 on v0

--- a/solution.py
+++ b/solution.py
@@ -111,7 +111,8 @@
         partial_moments = jnp.dot(
             local_weighted, explicit.reshape(node_local, cell_count), precision=PRECISE
         )
-        moments = lax.psum(partial_moments, "vert")
+        parts = lax.all_gather(partial_moments, "vert")
+        moments = jnp.sum(parts, axis=0)
         coeffs = jnp.dot(inverse, moments, precision=PRECISE)
         equilibrium = jnp.dot(invariants.T, coeffs, precision=PRECISE).reshape(current.shape)
         current = explicit - relax_share[None] * (explicit - equilibrium)

time: 241 us -> 211 us (0.88)
  blocking collectives: 101 us -> 69.7 us
    psum x2 -> x0, blocking collectives: 77.4 us -> none  [per_device(): moments = lax.psum(partial_moments, 'vert')]
    all_gather x0 -> x2, blocking collectives: none -> 46.1 us  [per_device(): parts = lax.all_gather(partial_moments, 'vert')]
  transfers between devices with their start and end apart: 6 -> 6, of which waited for: 2 -> 2; matrix products, arithmetic and copies ran while one was open for 9% -> 11% of each run, Pallas kernels for 0% -> 0%
where the time goes in v1:
time: 211 us
  waiting for transfers between devices  97 us (46%)
  blocking collectives  69.7 us (33%)
  local copies, waits for them, and re-layouts  18.6 us (9%)
  between operations  13.7 us (6%)
  other arithmetic  6.6 us (3%)
  matrix products  4.08 us (2%)
    all_gather x2, waiting for transfers between devices, per_device(): lax.all_gather(rounded.reshape(node_local, cell_count), 'vert', axis=0, t...  96.9 us
    all_gather x2, blocking collectives, per_device(): parts = lax.all_gather(partial_moments, 'vert')  46.1 us
    all_gather x1, blocking collectives, per_device(): all_weights = lax.all_gather(node_weight, 'vert', axis=0, tiled=True)  23.6 us
    gather x4, local copies, waits for them, and re-layouts, one_block(): picked = jnp.take(blocks, column_list, axis=0).reshape(-1, cell_count)  8.75 us
  transfers between devices with their start and end apart: 6, of which 2 were waited for; matrix products, arithmetic and copies ran while one was open for 11% of the time, Pallas kernels for 0%

profile of v1, /device:TPU:32, one launch (start us, length us, event | category | flops | bytes accessed | tf_op | source)
XLA Modules:
  0.0 210.9 jit_solution(3188532590383358306)
XLA Ops:
  6.5 1.1 copy.54
  7.6 0.5 collective-permute-start
  8.1 1.6 copy.68
  10.2 23.6 %all-gather.4 = f32[16,1,256]{2,1,0:T(1,128)S(1)} all-gather(f32[1,1,256]{2,1,0:T(1,128)} %bitcast.113), channel_id=1, replica_groups=mesh['gx'=32,'vert'=16] {'vert'}, dimensions={0}, use_global_device_ids=true | all-gather | bytes 17408 | tf_op jit(solution)/shard_map/all_gather | solution.py:91
  33.8 0.4 fusion.42
  34.2 0.5 cholesky.17
  34.8 0.6 compare_reduce_fusion
  35.4 0.6 fusion.57
  36.1 0.4 custom-call.10
  36.6 0.7 add_divide_fusion
  37.7 0.7 fusion.80
  38.5 36.6 %all-gather.10.cloned.1.call-done = bf16[4096,1,256]{2,0,1:T(8,128)(2,1)} async-done(((bf16[256,1,256]{2,0,1:T(8,128)(2,1)}), bf16[4096,1,256]{2,0,1:T(8,128)(2,1)}) %all-gather.10.cloned.1.call-update) | async-done | bytes 2097168 | tf_op jit(solution)/shard_map/all_gather | solution.py:103
  75.1 5.3 %while.20 = (s32[]{:T(128)}, f32[2,128,256]{2,1,0:T(8,128)S(1)}, bf16[2,128,1536]{2,1,0:T(8,128)(2,1)S(1)}, s32[2,12]{1,0:T(2,128)S(1)}, bf16[32,128,256]{2,1,0:T(8,128)(2,1)}, /*index=5*/s32[]{:T(128)}) while((s32[]{:T(128)}, f32[2,128,256]{2,1,0:T(8,128)S(1)}, bf16[2,128,1536]{2,1,0:T(8,128)(2,1)S(1)}, s32[2,12]{1,0:T(2,128)S(1)}, ...), condition=%wide.region_1.3_spmd, body=%wide.region_0.2_spmd.sunk | while | flops 101057608 | bytes 4461865 | solution.py:83
  75.1 2.2 %gather_fusion = bf16[12,128,256]{2,1,0:T(8,128)(2,1)S(1)} fusion(bf16[32,128,256]{2,1,0:T(8,128)(2,1)} %get-tuple-element.224, s32[1024]{0:T(1024)S(1)} %pad_clamp_fusion.4), kind=kCustom, calls=%fused_computation.clone.clone.1 | custom fusion | bytes 1572912 | tf_op jit(solution)/shard_map/while/body/eval_jaxpr/jit(_take)/gather | solution.py:80
  77.5 0.3 fusion.109
  77.8 2.2 %gather_fusion = bf16[12,128,256]{2,1,0:T(8,128)(2,1)S(1)} fusion(bf16[32,128,256]{2,1,0:T(8,128)(2,1)} %get-tuple-element.224, s32[1024]{0:T(1024)S(1)} %pad_clamp_fusion.4), kind=kCustom, calls=%fused_computation.clone.clone.1 | custom fusion | bytes 1572912 | tf_op jit(solution)/shard_map/while/body/eval_jaxpr/jit(_take)/gather | solution.py:80
  80.2 0.3 fusion.109
  80.6 1.4 fusion.22
  82.3 23.0 %all-gather.5 = f32[16,5,256]{2,1,0:T(8,128)S(1)} all-gather(f32[1,5,256]{2,1,0:T(8,128)S(1)} %convolution_bitcast_fusion.5), channel_id=3, replica_groups=mesh['gx'=32,'vert'=16] {'vert'}, dimensions={0}, use_global_device_ids=true | all-gather | bytes 87040 | tf_op jit(solution)/shard_map/all_gather | solution.py:114
  105.5 1.1 fusion.86
  106.6 0.5 collective-permute-start.2
  107.3 0.7 fusion.74
  108.0 60.3 %all-gather.12.cloned.1.call-done = bf16[4096,1,256]{0,2,1:T(8,128)(2,1)} async-done(((bf16[256,1,256]{0,2,1:T(8,128)(2,1)}), bf16[4096,1,256]{0,2,1:T(8,128)(2,1)}) %all-gather.12.cloned.1.call-update) | async-done | bytes 2097168 | tf_op jit(solution)/shard_map/all_gather | solution.py:103
  168.3 4.1 %copy.65 = bf16[4096,1,256]{2,0,1:T(8,128)(2,1)} copy(bf16[4096,1,256]{0,2,1:T(8,128)(2,1)} %all-gather.12.cloned.1.call-done) | data formatting | bytes 4194304 | tf_op jit(solution)/shard_map/while | solution.py:83
  172.4 5.3 %while.21 = (s32[]{:T(128)}, f32[2,128,256]{2,1,0:T(8,128)S(1)}, bf16[2,128,1536]{2,1,0:T(8,128)(2,1)S(1)}, s32[2,12]{1,0:T(2,128)S(1)}, bf16[32,128,256]{2,1,0:T(8,128)(2,1)}, /*index=5*/s32[]{:T(128)}) while((s32[]{:T(128)}, f32[2,128,256]{2,1,0:T(8,128)S(1)}, bf16[2,128,1536]{2,1,0:T(8,128)(2,1)S(1)}, s32[2,12]{1,0:T(2,128)S(1)}, ...), condition=%wide.region_6.8_spmd, body=%wide.region_5.7_spmd.sunk | while | flops 101057608 | bytes 4461865 | solution.py:83
  172.4 2.2 %gather_fusion.1 = bf16[12,128,256]{2,1,0:T(8,128)(2,1)S(1)} fusion(bf16[32,128,256]{2,1,0:T(8,128)(2,1)} %get-tuple-element.242, s32[1024]{0:T(1024)S(1)} %pad_clamp_fusion.5), kind=kCustom, calls=%fused_computation.1.clone.clone.1 | custom fusion | bytes 1572912 | tf_op jit(solution)/shard_map/while/body/eval_jaxpr/jit(_take)/gather | solution.py:80
  174.8 0.3 fusion.112
  175.1 2.2 %gather_fusion.1 = bf16[12,128,256]{2,1,0:T(8,128)(2,1)S(1)} fusion(bf16[32,128,256]{2,1,0:T(8,128)(2,1)} %get-tuple-element.242, s32[1024]{0:T(1024)S(1)} %pad_clamp_fusion.5), kind=kCustom, calls=%fused_computation.1.clone.clone.1 | custom fusion | bytes 1572912 | tf_op jit(solution)/shard_map/while/body/eval_jaxpr/jit(_take)/gather | solution.py:80
  177.9 1.4 fusion.34
  179.6 23.1 %all-gather.6 = f32[16,5,256]{2,1,0:T(8,128)S(1)} all-gather(f32[1,5,256]{2,1,0:T(8,128)S(1)} %convolution_bitcast_fusion.4), channel_id=5, replica_groups=mesh['gx'=32,'vert'=16] {'vert'}, dimensions={0}, use_global_device_ids=true | all-gather | bytes 87040 | tf_op jit(solution)/shard_map/all_gather | solution.py:114
  202.8 0.4 fusion.15
  203.3 0.8 copy.62
  (67 shorter events, 3.2 us)
Async XLA Ops:
  6.5 68.5 %all-gather.10.cloned.1.call-start = ((), (), s32[]{:S(2)}) async-start(), calls=%async_computation | async-start | bytes 2228224 | tf_op jit(solution)/shard_map/all_gather | solution.py:103
  7.6 73.0 %collective-permute-start.1 = (f32[256,1,256]{0,2,1:T(8,128)S(1)}, f32[256,1,256]{0,2,1:T(8,128)}, u32[]{:S(2)}, u32[]{:S(2)}) collective-permute-start(f32[256,1,256]{0,2,1:T(8,128)S(1)} %copy.54), channel_id=1, source_target_pairs={{16,0},{32,16},{48,32},{64,48},{80,64},{96,80},{112,96},{128,112},... | collective-permute-start | bytes 786440 | tf_op jit(solution)/shard_map/ppermute | solution.py:26
  7.6 73.0 %collective-permute-start = (f32[256,1,256]{0,2,1:T(8,128)S(1)}, f32[256,1,256]{0,2,1:T(8,128)}, u32[]{:S(2)}, u32[]{:S(2)}) collective-permute-start(f32[256,1,256]{0,2,1:T(8,128)S(1)} %copy.54), channel_id=1, source_target_pairs={{0,16},{16,32},{32,48},{48,64},{64,80},{80,96},{96,112},{112,128},... | collective-permute-start | bytes 786440 | tf_op jit(solution)/shard_map/ppermute | solution.py:23
  9.8 65.3 %copy-start = (bf16[2,128,1536]{2,1,0:T(8,128)(2,1)S(1)}, bf16[2,128,1536]{2,1,0:T(8,128)(2,1)}, u32[]{:S(2)}) copy-start(bf16[2,128,1536]{2,1,0:T(8,128)(2,1)} %param.14) | copy-start | bytes 2359300
  9.8 65.3 %copy-start.1 = (s32[2,12]{1,0:T(2,128)S(1)}, s32[2,12]{1,0:T(2,128)}, u32[]{:S(2)}) copy-start(s32[2,12]{1,0:T(2,128)} %param.15) | copy-start | bytes 292
  9.8 158.5 %all-gather.12.cloned.1.call-start = ((), (), s32[]{:S(2)}) async-start(), calls=%async_computation.1 | async-start | bytes 2228224 | tf_op jit(solution)/shard_map/all_gather | solution.py:103
  80.4 1.6 copy-start.2
  106.6 71.3 %collective-permute-start.3 = (f32[256,1,256]{0,2,1:T(8,128)S(1)}, f32[256,1,256]{0,2,1:T(8,128)}, u32[]{:S(2)}, u32[]{:S(2)}) collective-permute-start(f32[256,1,256]{0,2,1:T(8,128)S(1)} %get-tuple-element.127), channel_id=1, source_target_pairs={{16,0},{32,16},{48,32},{64,48},{80,64},{96,80},{112,96},{128,112},... | collective-permute-start | bytes 786440 | tf_op jit(solution)/shard_map/ppermute | solution.py:26
  106.6 71.3 %collective-permute-start.2 = (f32[256,1,256]{0,2,1:T(8,128)S(1)}, f32[256,1,256]{0,2,1:T(8,128)}, u32[]{:S(2)}, u32[]{:S(2)}) collective-permute-start(f32[256,1,256]{0,2,1:T(8,128)S(1)} %get-tuple-element.127), channel_id=1, source_target_pairs={{0,16},{16,32},{32,48},{48,64},{64,80},{80,96},{96,112},{112,128},... | collective-permute-start | bytes 786440 | tf_op jit(solution)/shard_map/ppermute | solution.py:23
Sparse Core Ops, SparseCore 0:
  10.4 64.6 all-gather.9
  106.7 61.5 all-gather.11
